TPU v7x, 128 devices: a whole 4x4x4 slice. The times are simulated.
128 devices in a mesh: dp: 128 (over x, y, z, core).
Axes of the slice: x: 4, y: 4, z: 4, core: 2. Of those that a mesh axis runs over, the one named last changes fastest.
Arguments:
- hidden_in: bfloat16 [131072, 1024], P('dp'), may hold values from -15 to 15
- lengths: int32 [128, 8], P('dp'), may hold values from 1 to 512, 1024 in all within a row
- owner: int32 [1024], P('dp'), may hold values from 0 to 1023, each once
- pooled_grad: float32 [1024, 1024], P('dp'), may hold values from -6 to 6
- norm_gain: bfloat16 [1024], replicated, may hold values from 0.25 to 1.75
- w_query: bfloat16 [1024, 2048], replicated
- w_key: bfloat16 [1024, 1024], P('dp')
- value_weight: bfloat16 [1024, 1024], P('dp'), may hold values from -0.1875 to 0.1875
- w_out: bfloat16 [2048, 1024], replicated, may hold values from -0.125 to 0.125
Outputs:
- grad_in: bfloat16 [131072, 1024], P('dp')
- grad_key: float32 [1024, 1024], P('dp')
- grad_value: float32 [1024, 1024], P('dp')
- grad_gain: float32 [1024], replicated
Inputs may be any that keep to these rules, and one draw needn't show every extreme that they name: Each row of lengths sums to 1024, and some statement has exactly 512 tokens. `owner`: a permutation.
All inputs are finite; a program needn't handle non-finite values.
Results may differ from a plain program's by a relative error of at most 0.035.
The roundings to bfloat16 on the way count: a program that leaves them out, or rounds other values in their place, can miss the bound.
Values may be sent and summed in bfloat16 or wider, within the bound.
A program may use at most 128 MiB of HBM per device.

v0:
```python
import jax
import jax.numpy as jnp
from jax import lax
from jax.sharding import PartitionSpec as P

QUERY_HEADS = 16
KEY_HEADS = 8
HEAD_WIDTH = 128


def per_device(
    hidden_in, lengths, owner, pooled_grad, norm_gain, w_query, w_key, value_weight, w_out
):
    token_rows = hidden_in.shape[0]
    statement_slots = lengths.shape[1]
    key_value_width = w_key.shape[1]
    head_groups = QUERY_HEADS // KEY_HEADS
    scale_q = 1.0 / HEAD_WIDTH**0.5
    every_grad = lax.all_gather(pooled_grad.astype(jnp.bfloat16), "dp", axis=0, tiled=True).astype(
        pooled_grad.dtype
    )
    cached = jnp.take(every_grad, owner, axis=0)
    inputs_f = hidden_in.astype(jnp.float32)
    inv_rms = lax.rsqrt(jnp.mean(inputs_f * inputs_f, axis=-1, keepdims=True) + 1e-06)
    normed = inputs_f * inv_rms
    normed_b = (normed * norm_gain.astype(jnp.float32)).astype(jnp.bfloat16)
    kv_rows = jnp.concatenate([w_key, value_weight], axis=1)
    kv_full = lax.all_gather(kv_rows, "dp", axis=0, tiled=True)
    key_value_joint = jnp.dot(normed_b, kv_full, preferred_element_type=jnp.float32)
    key_value_joint = key_value_joint.astype(jnp.bfloat16)
    key_rows = key_value_joint[:, :key_value_width].reshape(token_rows, KEY_HEADS, HEAD_WIDTH)
    value_rows = key_value_joint[:, key_value_width:].reshape(token_rows, KEY_HEADS, HEAD_WIDTH)
    ends = jnp.cumsum(lengths[0])
    last_rows = ends - 1
    positions = jnp.arange(token_rows, dtype=jnp.int32)
    segment = jnp.sum((positions[:, None] >= ends[None, :]).astype(jnp.int32), axis=1)
    member = segment[None, :] == jnp.arange(statement_slots, dtype=jnp.int32)[:, None]
    last_normed = jnp.take(normed_b, last_rows, axis=0)
    query_rows = jnp.dot(last_normed, w_query, preferred_element_type=jnp.float32).astype(
        jnp.bfloat16
    )
    query_rows = query_rows.reshape(statement_slots, KEY_HEADS, head_groups, HEAD_WIDTH)
    scores = (
        jnp.einsum("sgqe,tge->sgqt", query_rows, key_rows, preferred_element_type=jnp.float32)
        * scale_q
    )
    scores = jnp.where(member[:, None, None, :], scores, -1e30)
    top = jnp.max(scores, axis=-1, keepdims=True)
    expo = jnp.exp(scores - top)
    probs = expo / jnp.sum(expo, axis=-1, keepdims=True)
    probs_b = probs.astype(jnp.bfloat16)
    attended = jnp.einsum(
        "sgqt,tge->sgqe", probs_b, value_rows, preferred_element_type=jnp.float32
    ).astype(jnp.bfloat16)
    attended = attended.reshape(statement_slots, QUERY_HEADS * HEAD_WIDTH)
    pooled = jnp.take(inputs_f, last_rows, axis=0) + jnp.dot(
        attended, w_out, preferred_element_type=jnp.float32
    )
    inv_len = lax.rsqrt(jnp.sum(pooled * pooled, axis=-1, keepdims=True) + 1e-06)
    embed = pooled * inv_len
    grad_pool = inv_len * (cached - embed * jnp.sum(embed * cached, axis=-1, keepdims=True))
    grad_pool_b = grad_pool.astype(jnp.bfloat16)
    attention_gradient = lax.dot_general(
        grad_pool_b, w_out, (((1,), (1,)), ((), ())), preferred_element_type=jnp.float32
    )
    attention_gradient = attention_gradient.astype(jnp.bfloat16).reshape(
        statement_slots, KEY_HEADS, head_groups, HEAD_WIDTH
    )
    grad_values = jnp.einsum(
        "sgqt,sgqe->tge", probs_b, attention_gradient, preferred_element_type=jnp.float32
    )
    grad_values = grad_values.astype(jnp.bfloat16).reshape(token_rows, key_value_width)
    grad_prob = jnp.einsum(
        "sgqe,tge->sgqt", attention_gradient, value_rows, preferred_element_type=jnp.float32
    )
    grad_score = probs * (grad_prob - jnp.sum(probs * grad_prob, axis=-1, keepdims=True)) * scale_q
    grad_score = grad_score.astype(jnp.bfloat16)
    grad_query = jnp.einsum(
        "sgqt,tge->sgqe", grad_score, key_rows, preferred_element_type=jnp.float32
    )
    grad_query = grad_query.astype(jnp.bfloat16).reshape(statement_slots, QUERY_HEADS * HEAD_WIDTH)
    grad_keys = jnp.einsum(
        "sgqt,sgqe->tge", grad_score, query_rows, preferred_element_type=jnp.float32
    )
    grad_keys = grad_keys.astype(jnp.bfloat16).reshape(token_rows, key_value_width)
    grad_both = jnp.concatenate([grad_keys, grad_values], axis=1)
    grad_normed = lax.dot_general(
        grad_both, kv_full, (((1,), (1,)), ((), ())), preferred_element_type=jnp.float32
    )
    query_back = lax.dot_general(
        grad_query, w_query, (((1,), (1,)), ((), ())), preferred_element_type=jnp.float32
    )
    grad_normed = grad_normed.at[last_rows].add(query_back)
    gain_total = lax.psum(jnp.sum(grad_normed * normed, axis=0), "dp")
    scaled = grad_normed * norm_gain.astype(jnp.float32)
    grad_in = inv_rms * (scaled - normed * jnp.mean(scaled * normed, axis=-1, keepdims=True))
    grad_in = grad_in.at[last_rows].add(grad_pool).astype(jnp.bfloat16)
    weight_share = lax.psum_scatter(
        lax.dot_general(
            normed_b, grad_both, (((0,), (0,)), ((), ())), preferred_element_type=jnp.float32
        ),
        "dp",
        scatter_dimension=0,
        tiled=True,
    )
    return (
        grad_in,
        weight_share[:, :key_value_width],
        weight_share[:, key_value_width:],
        gain_total,
    )


def solution(mesh):
    return jax.shard_map(
        per_device,
        mesh=mesh,
        in_specs=(
            P("dp", None),
            P("dp", None),
            P("dp"),
            P("dp", None),
            P(),
            P(),
            P("dp", None),
            P("dp", None),
            P(),
        ),
        out_specs=(P("dp", None), P("dp", None), P("dp", None), P()),
        check_vma=False,
    )
```

profile of v0, /device:TPU:0, one launch (start us, length us, event | category | flops | bytes accessed | tf_op | source)
XLA Modules:
  0.0 839.9 jit_solution(15867571985289667130)
XLA Ops:
  7.2 1.5 convert_element_type.73
  8.8 1.4 pad_maximum_fusion.3
  10.9 4.0 convert_element_type.64
  15.6 1.9 multiply_convert_fusion
  17.5 2.4 gather_fusion
  19.9 2.8 gather_fusion.1
  22.9 2.9 convolution_convert_fusion.2
  25.8 53.7 %all-gather.5.cloned.1.call-done = bf16[1024,1024]{1,0:T(8,128)(2,1)} async-done(((bf16[8,1024]{1,0:T(8,128)(2,1)}), bf16[1024,1024]{1,0:T(8,128)(2,1)}) %all-gather.5.cloned.1.call-update) | async-done | bytes 2097168 | tf_op jit(solution)/shard_map/all_gather | solution.py:19
  79.5 4.0 convert_element_type.74
  83.5 2.8 gather_fusion.2
  86.3 61.3 %all-gather.3.cloned.1.call-done = bf16[1024,2048]{1,0:T(8,128)(2,1)} async-done(((bf16[8,2048]{1,0:T(8,128)(2,1)}), bf16[1024,2048]{1,0:T(8,128)(2,1)}) %all-gather.3.cloned.1.call-update) | async-done | bytes 4194320 | tf_op jit(solution)/shard_map/all_gather | solution.py:28
  147.6 7.3 convolution_convert_fusion
  154.9 1.2 slice_bitcast_fusion.1
  156.1 2.0 copy.35
  158.1 2.0 copy.36
  160.1 2.4 fusion.58
  162.5 2.3 fusion.33
  166.3 1.2 convolution_convert_fusion.1
  168.2 2.1 bitcast_convert_fusion
  170.3 2.8 bitcast_convert_fusion.1
  173.1 10.6 %fusion.2 = f32[1024,2048]{1,0:T(8,128)} fusion(bf16[1024,1024]{1,0:T(8,128)(2,1)} %multiply_convert_fusion, bf16[1024,1024]{0,1:T(8,128)(2,1)} %bitcast.63, bf16[1024,1024]{0,1:T(8,128)(2,1)} %bitcast.75), kind=kOutput, calls=%fused_computation.16 | convolution fusion | flops 4303355904 | bytes 14680064 | tf_op jit(solution)/shard_map/dot_general | solution.py:99
  183.7 2.4 fusion.30
  186.1 3.5 fusion.61
  189.6 8.4 %fusion.3 = f32[1024,1024]{1,0:T(8,128)} fusion(bf16[1024,2048]{1,0:T(8,128)(2,1)} %all-gather.3.cloned.1.call-done, bf16[1024,1024]{0,1:T(8,128)(2,1)S(1)} %bitcast.64, bf16[1024,1024]{0,1:T(8,128)(2,1)S(1)} %bitcast.76), kind=kOutput, calls=%fused_computation.17 | convolution fusion | flops 4303355904 | bytes 12582912 | tf_op jit(solution)/shard_map/dot_general | solution.py:87
  198.1 4.8 scatter_fusion
  202.8 3.5 multiply_reduce_fusion
  206.3 2.9 subtract_multiply_fusion
  209.3 4.9 scatter_custom_fusion.1
  214.1 3.8 convert_element_type.84
  218.0 64.0 %psum.7 = f32[1024]{0:T(1024)} all-reduce(f32[1024]{0:T(1024)S(1)} %get-tuple-element.5), channel_id=1, replica_groups=mesh['dp'=128] {'dp'}, use_global_device_ids=true, to_apply=%region_13.15 | all-reduce | flops 1024 | bytes 8192 | tf_op jit(solution)/shard_map/psum | solution.py:94
  282.0 550.0 %reduce-scatter.2.cloned.1.call-done = f32[8,2048]{1,0:T(8,128)} async-done(((f32[1024,2048]{1,0:T(8,128)}), f32[8,2048]{1,0:T(8,128)}) %reduce-scatter.2.cloned.1.call-update) | async-done | bytes 65552 | tf_op jit(solution)/shard_map/reduce_scatter | solution.py:98
  831.9 1.4 fusion.57
  (40 shorter events, 3.9 us)
Async XLA Ops:
  7.2 7.9 copy-start
  7.2 7.7 copy-start.5
  7.2 72.3 %all-gather.5.cloned.1.call-start = ((), (), s32[]{:S(2)}) async-start(), calls=%async_computation.2 | async-start | bytes 2113536 | tf_op jit(solution)/shard_map/all_gather | solution.py:19
  8.8 138.8 %all-gather.3.cloned.1.call-start = ((), (), s32[]{:S(2)}) async-start(), calls=%async_computation.1 | async-start | bytes 4227072 | tf_op jit(solution)/shard_map/all_gather | solution.py:28
  10.2 821.8 %reduce-scatter.2.cloned.1.call-start = ((), (), s32[]{:S(2)}) async-start(), calls=%async_computation.3 | async-start | bytes 8454144 | tf_op jit(solution)/shard_map/reduce_scatter | solution.py:98
  14.9 7.8 copy-start.6
  162.5 2.8 copy-start.2
  165.3 2.2 copy-start.4
  186.1 3.5 copy-start.3
  186.1 3.5 copy-start.7
  202.8 3.5 copy-start.1
Sparse Core Ops, SparseCore 0:
  11.7 67.7 all-gather.4
  83.2 64.2 all-gather.2
  183.8 648.0 reduce-scatter.1
where the time goes:
time: 841 us; the launch traced here: 840 us
  waiting for transfers between devices  665 us (79%)
  blocking collectives  64 us (8%)
  matrix products  47.4 us (6%)
  other arithmetic  34.3 us (4%)
  local copies, waits for them, and re-layouts  15.1 us (2%)
  between operations  13.9 us (2%)
    reduce_scatter x1, waiting for transfers between devices, per_device(): lax.psum_scatter(lax.dot_general(normed_b, grad_both, (((0,), (0,)), ((),...  550 us
    psum x1, blocking collectives, per_device(): gain_total = lax.psum(jnp.sum(grad_normed * normed, axis=0), 'dp')  64 us
    all_gather x1, waiting for transfers between devices, per_device(): kv_full = lax.all_gather(kv_rows, 'dp', axis=0, tiled=True)  61.3 us
    all_gather x1, waiting for transfers between devices, per_device(): lax.all_gather(pooled_grad.astype(jnp.bfloat16), 'dp', axis=0, tiled=True)  53.7 us
  transfers between devices with their start and end apart: 3, of which 3 were waited for; matrix products, arithmetic and copies ran while one was open for 7% of the time, Pallas kernels for 0%

commit v1 on v0

--- a/solution.py
+++ b/solution.py
@@ -2,6 +2,7 @@
 import jax.numpy as jnp
 from jax import lax
 from jax.sharding import PartitionSpec as P
+from jax.lax import all_to_all, axis_size
 
 QUERY_HEADS = 16
 KEY_HEADS = 8
@@ -16,9 +17,15 @@
     key_value_width = w_key.shape[1]
     head_groups = QUERY_HEADS // KEY_HEADS
     scale_q = 1.0 / HEAD_WIDTH**0.5
-    every_grad = lax.all_gather(pooled_grad.astype(jnp.bfloat16), "dp", axis=0, tiled=True).astype(
-        pooled_grad.dtype
-    )
+    every_grad = jnp.concatenate(
+        all_to_all(
+            jnp.stack(axis_size("dp") * [pooled_grad.astype(jnp.bfloat16)], 0),
+            axis_name="dp",
+            split_axis=0,
+            concat_axis=0,
+        ),
+        0,
+    ).astype(pooled_grad.dtype)
     cached = jnp.take(every_grad, owner, axis=0)
     inputs_f = hidden_in.astype(jnp.float32)
     inv_rms = lax.rsqrt(jnp.mean(inputs_f * inputs_f, axis=-1, keepdims=True) + 1e-06)

time: 841 us -> 789 us (0.938)
  waiting for transfers between devices: 665 us -> 603 us
  starting transfers between devices: 0.12 us -> 11.8 us
    all_gather x1 -> x0, waiting for transfers between devices: 53.7 us -> none  [per_device(): lax.all_gather(pooled_grad.astype(jnp.bfloat16), 'dp', axis=0, tiled=True)]
    all_gather x1, waiting for transfers between devices: 61.3 us -> 35.4 us  [per_device(): kv_full = lax.all_gather(kv_rows, 'dp', axis=0, tiled=True)]
    all_to_all x0 -> x1, waiting for transfers between devices: none -> 17 us  [per_device(): all_to_all(jnp.stack(axis_size('dp') * [pooled_grad.astype(jnp.bfloat16)]...]
    all_to_all x0 -> x1, starting transfers between devices: none -> 11.7 us  [per_device(): all_to_all(jnp.stack(axis_size('dp') * [pooled_grad.astype(jnp.bfloat16)]...]
where the time goes in v1:
time: 789 us
  waiting for transfers between devices  603 us (76%)
  blocking collectives  64.1 us (8%)
  matrix products  47.4 us (6%)
  other arithmetic  31.5 us (4%)
  local copies, waits for them, and re-layouts  16.7 us (2%)
  between operations  14.2 us (2%)
  starting transfers between devices  11.8 us (1%)
    reduce_scatter x1, waiting for transfers between devices, per_device(): lax.psum_scatter(lax.dot_general(normed_b, grad_both, (((0,), (0,)), ((),...  551 us
    psum x1, blocking collectives, per_device(): gain_total = lax.psum(jnp.sum(grad_normed * normed, axis=0), 'dp')  64.1 us
    all_gather x1, waiting for transfers between devices, per_device(): kv_full = lax.all_gather(kv_rows, 'dp', axis=0, tiled=True)  35.4 us
    all_to_all x1, waiting for transfers between devices, per_device(): all_to_all(jnp.stack(axis_size('dp') * [pooled_grad.astype(jnp.bfloat16)]...  17 us
  transfers between devices with their start and end apart: 3, of which 3 were waited for; matrix products, arithmetic and copies ran while one was open for 7% of the time, Pallas kernels for 0%

profile of v1, /device:TPU:0, one launch (start us, length us, event | category | flops | bytes accessed | tf_op | source)
XLA Modules:
  0.0 788.6 jit_solution(6064195615085665747)
XLA Ops:
  7.2 1.5 pad_maximum_fusion.3
  9.5 1.6 stack.2
  11.1 11.7 %all-to-all-start = ((bf16[128,8,1024]{2,1,0:T(8,128)(2,1)}), bf16[128,8,1024]{2,1,0:T(8,128)(2,1)}, u32[]{:S(2)}, u32[]{:S(2)}) async-start(bf16[128,8,1024]{2,1,0:T(8,128)(2,1)} %stack.2), calls=%async_computation | async-start | bytes 4194304 | tf_op jit(solution)/shard_map/all_to_all | solution.py:21
  22.9 2.5 convert_element_type.67
  26.1 1.9 multiply_convert_fusion
  28.0 2.4 gather_fusion
  30.5 2.8 gather_fusion.1
  33.4 2.9 convolution_convert_fusion.2
  36.3 17.0 %all-to-all-done = bf16[128,8,1024]{2,1,0:T(8,128)(2,1)} async-done(((bf16[128,8,1024]{2,1,0:T(8,128)(2,1)}), bf16[128,8,1024]{2,1,0:T(8,128)(2,1)}, u32[]{:S(2)}, u32[]{:S(2)}) %all-to-all-start) | async-done | bytes 2097184 | tf_op jit(solution)/shard_map/all_to_all | solution.py:21
  53.2 4.1 bitcast_convert_fusion.2
  57.3 2.8 gather_fusion.2
  60.1 35.4 %all-gather.2.cloned.1.call-done = bf16[1024,2048]{1,0:T(8,128)(2,1)} async-done(((bf16[8,2048]{1,0:T(8,128)(2,1)}), bf16[1024,2048]{1,0:T(8,128)(2,1)}) %all-gather.2.cloned.1.call-update) | async-done | bytes 4194320 | tf_op jit(solution)/shard_map/all_gather | solution.py:35
  95.5 7.3 convolution_convert_fusion
  104.0 2.0 copy.35
  106.0 1.9 copy.36
  107.9 2.4 fusion.58
  110.4 2.3 fusion.33
  114.2 1.2 convolution_convert_fusion.1
  116.0 2.1 bitcast_convert_fusion
  118.1 2.8 bitcast_convert_fusion.1
  120.9 10.7 %fusion.2 = f32[1024,2048]{1,0:T(8,128)} fusion(bf16[1024,1024]{1,0:T(8,128)(2,1)} %multiply_convert_fusion, bf16[1024,1024]{0,1:T(8,128)(2,1)} %bitcast.66, bf16[1024,1024]{0,1:T(8,128)(2,1)} %bitcast.78), kind=kOutput, calls=%fused_computation.16 | convolution fusion | flops 4303355904 | bytes 14680064 | tf_op jit(solution)/shard_map/dot_general | solution.py:106
  131.6 2.4 fusion.30
  134.0 3.5 fusion.61
  137.5 8.4 %fusion.3 = f32[1024,1024]{1,0:T(8,128)} fusion(bf16[1024,2048]{1,0:T(8,128)(2,1)} %all-gather.2.cloned.1.call-done, bf16[1024,1024]{0,1:T(8,128)(2,1)S(1)} %bitcast.67, bf16[1024,1024]{0,1:T(8,128)(2,1)S(1)} %bitcast.79), kind=kOutput, calls=%fused_computation.17 | convolution fusion | flops 4303355904 | bytes 12582912 | tf_op jit(solution)/shard_map/dot_general | solution.py:94
  145.9 4.8 scatter_fusion
  150.7 3.5 multiply_reduce_fusion
  154.2 2.9 subtract_multiply_fusion
  157.1 4.8 scatter_custom_fusion.1
  161.9 3.8 convert_element_type.88
  165.7 64.1 %psum.7 = f32[1024]{0:T(1024)} all-reduce(f32[1024]{0:T(1024)S(1)} %get-tuple-element.5), channel_id=1, replica_groups=mesh['dp'=128] {'dp'}, use_global_device_ids=true, to_apply=%region_13.15 | all-reduce | flops 1024 | bytes 8192 | tf_op jit(solution)/shard_map/psum | solution.py:101
  229.8 550.5 %reduce-scatter.2.cloned.1.call-done = f32[8,2048]{1,0:T(8,128)} async-done(((f32[1024,2048]{1,0:T(8,128)}), f32[8,2048]{1,0:T(8,128)}) %reduce-scatter.2.cloned.1.call-update) | async-done | bytes 65552 | tf_op jit(solution)/shard_map/reduce_scatter | solution.py:105
  780.4 1.4 fusion.57
  (42 shorter events, 5.1 us)
Async XLA Ops:
  7.2 15.7 %copy-start.5 = (bf16[1024]{0:T(1024)(128)(2,1)S(1)}, bf16[1024]{0:T(1024)(128)(2,1)}, u32[]{:S(2)}) copy-start(bf16[1024]{0:T(1024)(128)(2,1)} %param.15) | copy-start | bytes 6148
  7.2 15.7 %copy-start = (bf16[1024,1024]{1,0:T(8,128)(2,1)S(1)}, bf16[1024,1024]{1,0:T(8,128)(2,1)}, u32[]{:S(2)}) copy-start(bf16[1024,1024]{1,0:T(8,128)(2,1)} %param.11) | copy-start | bytes 6291460
  7.2 88.3 %all-gather.2.cloned.1.call-start = ((), (), s32[]{:S(2)}) async-start(), calls=%async_computation.2 | async-start | bytes 4227072 | tf_op jit(solution)/shard_map/all_gather | solution.py:35
  11.1 42.1 %all-to-all-start = ((bf16[128,8,1024]{2,1,0:T(8,128)(2,1)}), bf16[128,8,1024]{2,1,0:T(8,128)(2,1)}, u32[]{:S(2)}, u32[]{:S(2)}) async-start(bf16[128,8,1024]{2,1,0:T(8,128)(2,1)} %stack.2), calls=%async_computation | async-start | bytes 4194304 | tf_op jit(solution)/shard_map/all_to_all | solution.py:21
  22.8 2.6 copy-start.6
  22.8 757.6 %reduce-scatter.2.cloned.1.call-start = ((), (), s32[]{:S(2)}) async-start(), calls=%async_computation.3 | async-start | bytes 8454144 | tf_op jit(solution)/shard_map/reduce_scatter | solution.py:105
  25.4 7.9 copy-start.7
  110.4 2.8 copy-start.2
  113.2 2.2 copy-start.4
  134.0 3.5 copy-start.3
  134.0 3.5 copy-start.8
  150.7 3.5 copy-start.1
Sparse Core Ops, SparseCore 0:
  11.8 83.6 all-gather.1
  131.7 648.5 reduce-scatter.1
